TPU v7x, 128 devices: a whole 4x4x4 slice. The times are simulated.
128 devices in a mesh: row: 8 (over z, core), col: 16 (over x, y).
Axes of the slice: x: 4, y: 4, z: 4, core: 2. Of those that a mesh axis runs over, the one named last changes fastest.
Arguments:
- layer_input: bfloat16 [1024, 8192], P('col', 'row'), may hold values from -6 to 6
- out_grad: bfloat16 [1024, 8192], P('col', 'row'), may hold values from -6 to 6
- gate_saved: bfloat16 [1024, 14336], P('row', 'col'), may hold values from -8 to 8
- up_saved: bfloat16 [1024, 14336], P('row', 'col'), may hold values from -6 to 6
- gate_weight: bfloat16 [8192, 14336], P('row', 'col'), may hold values from -0.0625 to 0.0625
- up_weight: bfloat16 [8192, 14336], P('row', 'col'), may hold values from -0.0625 to 0.0625
- down_weight: bfloat16 [14336, 8192], P('col', 'row'), may hold values from -0.046875 to 0.046875
Outputs:
- input_grad: bfloat16 [1024, 8192], P('col', 'row')
- gate_weight_grad: float32 [8192, 14336], P('row', 'col')
- up_weight_grad: float32 [8192, 14336], P('row', 'col')
- down_weight_grad: float32 [14336, 8192], P('col', 'row')
All inputs are finite; a program needn't handle non-finite values.
Results may differ from a plain program's by a relative error of at most 0.02.
Values may be sent and summed in bfloat16 or wider, within the bound.
A program may use at most 128 MiB of HBM per device.

v0:
```python
import jax
import jax.numpy as jnp
from jax import lax
from jax.sharding import PartitionSpec as P


def in_one_piece(arrays, axis, dim, along):
    ends, at = ([], 0)
    for a in arrays[:-1]:
        at += a.shape[along]
        ends.append(at)
    both = jnp.concatenate(arrays, axis=along)
    return tuple(jnp.split(lax.all_gather(both, axis, axis=dim, tiled=True), ends, axis=along))


def cut_along(array, dim, peers):
    lengths = array.shape
    tiles = array.reshape(*lengths[:dim], peers, lengths[dim] // peers, *lengths[dim + 1 :])
    return jnp.moveaxis(tiles, dim, 0)


def sent_and_summed(array, axis, dim):
    peers = lax.axis_size(axis)
    tiles = lax.all_to_all(cut_along(array, dim, peers), axis, 0, 0, tiled=True)
    return jnp.sum(tiles.astype(jnp.float32), axis=0)


def contract_last(left, right):
    return lax.dot_general(
        left, right, (((1,), (1,)), ((), ())), preferred_element_type=jnp.float32
    )


def contract_first(left, right):
    return lax.dot_general(
        left, right, (((0,), (0,)), ((), ())), preferred_element_type=jnp.float32
    )


def swiglu_backward(hidden_grad, gate_saved, up_saved):
    gate_val = gate_saved.astype(jnp.float32)
    up_val = up_saved.astype(jnp.float32)
    sigma = 1.0 / (1.0 + jnp.exp(-gate_val))
    silu_val = gate_val * sigma
    hidden = (silu_val * up_val).astype(jnp.bfloat16)
    gate_grad = (hidden_grad * up_val * sigma * (1.0 + gate_val * (1.0 - sigma))).astype(
        jnp.bfloat16
    )
    up_grad = (hidden_grad * silu_val).astype(jnp.bfloat16)
    return (hidden, gate_grad, up_grad)


def shards(layer_input, out_grad, gate_saved, up_saved, gate_weight, up_weight, down_weight):
    input_all, grad_all = in_one_piece((layer_input, out_grad), "col", 0, 1)
    total_tokens = input_all.shape[0]
    hidden_grad = sent_and_summed(
        contract_last(grad_all, down_weight).astype(jnp.bfloat16), "row", 0
    )
    hidden, gate_grad, up_grad = swiglu_backward(hidden_grad, gate_saved, up_saved)
    hidden_all, gate_grad_all, up_grad_all = in_one_piece((hidden, gate_grad, up_grad), "row", 0, 1)
    input_grad = sent_and_summed(
        (contract_last(gate_grad_all, gate_weight) + contract_last(up_grad_all, up_weight)).astype(
            jnp.bfloat16
        ),
        "col",
        0,
    ).astype(jnp.bfloat16)
    scale = float(total_tokens) ** (-0.5)
    gate_weight_grad = scale * contract_first(input_all, gate_grad_all)
    up_weight_grad = scale * contract_first(input_all, up_grad_all)
    down_weight_grad = scale * contract_first(hidden_all, grad_all)
    return (input_grad, gate_weight_grad, up_weight_grad, down_weight_grad)


def solution(mesh):
    placed = (
        P("col", "row"),
        P("col", "row"),
        P("row", "col"),
        P("row", "col"),
        P("row", "col"),
        P("row", "col"),
        P("col", "row"),
    )
    return jax.shard_map(
        shards,
        mesh=mesh,
        in_specs=placed,
        out_specs=(P("col", "row"), P("row", "col"), P("row", "col"), P("col", "row")),
        check_vma=False,
    )
```

profile of v0, /device:TPU:0, one launch (start us, length us, event | category | flops | bytes accessed | tf_op | source)
XLA Modules:
  0.0 191.8 jit_solution(11499294929850534873)
XLA Ops:
  7.2 0.0 copy-start
  7.2 0.0 all-gather.3.cloned.1.call-start
  7.2 1.8 pad_maximum_fusion.1
  9.0 0.0 all-gather.3.cloned.1.call-update
  9.1 0.0 all-gather.5.cloned.1.call-start
  9.1 55.4 %all-gather.3.cloned.1.call-done = bf16[1024,2048]{1,0:T(8,128)(2,1)} async-done(((bf16[64,2048]{1,0:T(8,128)(2,1)}), bf16[1024,2048]{1,0:T(8,128)(2,1)}) %all-gather.3.cloned.1.call-update) | async-done | bytes 4194320 | tf_op jit(solution)/shard_map/all_gather | solution.py:13
  64.5 4.5 %fusion.6 = bf16[1024,896]{1,0:T(8,128)(2,1)S(1)} fusion(bf16[896,1024]{1,0:T(8,128)(2,1)} %param.13, bf16[1024,2048]{1,0:T(8,128)(2,1)} %all-gather.3.cloned.1.call-done), kind=kOutput, calls=%fused_computation.11 | convolution fusion | flops 1879965696 | bytes 5767168 | tf_op jit(solution)/shard_map/dot_general | solution.py:29
  69.0 0.0 copy-start.1
  69.0 0.0 copy-start.2
  69.0 28.8 %all_to_all.10 = bf16[8,128,896]{2,1,0:T(8,128)(2,1)S(1)} all-to-all(bf16[8,128,896]{2,1,0:T(8,128)(2,1)S(1)} %bitcast.6), channel_id=1, replica_groups=mesh['row'=8,'col'=16] {'row'}, dimensions={0} | all-to-all | bytes 3670016 | tf_op jit(solution)/shard_map/all_to_all | solution.py:24
  97.8 0.3 convert_reduce_fusion
  98.1 0.3 fusion.17
  98.4 0.9 pad_maximum_fusion
  99.3 0.0 all-gather.5.cloned.1.call-update
  99.3 35.6 %all-gather.5.cloned.1.call-done = bf16[1024,2688]{1,0:T(8,128)(2,1)} async-done(((bf16[128,2688]{1,0:T(8,128)(2,1)}), bf16[1024,2688]{1,0:T(8,128)(2,1)}) %all-gather.5.cloned.1.call-update) | async-done | bytes 5505040 | tf_op jit(solution)/shard_map/all_gather | solution.py:13
  134.9 4.0 %fusion.12 = f32[1024,1024]{1,0:T(8,128)S(1)} fusion(bf16[1024,896]{1,0:T(8,128)(2,1)S(1)} %copy-done, bf16[1024,2688]{1,0:T(8,128)(2,1)} %all-gather.5.cloned.1.call-done), kind=kOutput, calls=%fused_computation.15 | convolution fusion | flops 1879048192 | bytes 7864320 | tf_op jit(solution)/shard_map/dot_general | solution.py:29
  138.9 5.3 %add_convert_fusion = bf16[1024,1024]{1,0:T(8,128)(2,1)} fusion(f32[1024,1024]{1,0:T(8,128)S(1)} %fusion.12, bf16[1024,896]{1,0:T(8,128)(2,1)S(1)} %copy-done.4, bf16[1024,2688]{1,0:T(8,128)(2,1)} %all-gather.5.cloned.1.call-done), kind=kOutput, calls=%fused_computation | convolution fusion | flops 1881145344 | bytes 9961472 | tf_op jit(solution)/shard_map/dot_general | solution.py:29
  144.3 7.0 %all-to-all-start.1 = ((bf16[16,64,1024]{2,1,0:T(8,128)(2,1)}), bf16[16,64,1024]{2,1,0:T(8,128)(2,1)}, u32[]{:S(2)}, u32[]{:S(2)}) async-start(bf16[16,64,1024]{2,1,0:T(8,128)(2,1)} %bitcast.5), calls=%async_computation.1 | async-start | bytes 4194304 | tf_op jit(solution)/shard_map/all_to_all | solution.py:24
  151.3 0.0 slice-start.1
  151.3 6.2 %convolution_multiply_fusion = f32[896,1024]{1,0:T(8,128)} fusion(bf16[1024,2048]{1,0:T(8,128)(2,1)} %all-gather.3.cloned.1.call-done, bf16[1024,2688]{1,0:T(8,128)(2,1)} %all-gather.5.cloned.1.call-done), kind=kOutput, calls=%fused_computation.2 | convolution fusion | flops 1879965696 | bytes 7602176 | tf_op jit(solution)/shard_map/dot_general | solution.py:35
  157.5 4.3 %convolution_multiply_fusion.1 = f32[1024,896]{1,0:T(8,128)} fusion(bf16[1024,2048]{1,0:T(8,128)(2,1)S(1)} %copy-done.3, bf16[1024,2688]{1,0:T(8,128)(2,1)S(1)} %bitcast.8), kind=kOutput, calls=%fused_computation.3 | convolution fusion | flops 1879965696 | bytes 7602176 | tf_op jit(solution)/shard_map/dot_general | solution.py:35
  161.8 4.3 %convolution_multiply_fusion.2 = f32[1024,896]{1,0:T(8,128)} fusion(bf16[1024,2048]{1,0:T(8,128)(2,1)S(1)} %copy-done.3, bf16[1024,2688]{1,0:T(8,128)(2,1)S(1)} %bitcast.8), kind=kOutput, calls=%fused_computation.4 | convolution fusion | flops 1879965696 | bytes 7602176 | tf_op jit(solution)/shard_map/dot_general | solution.py:35
  166.1 16.2 %all-to-all-done.1 = bf16[16,64,1024]{2,1,0:T(8,128)(2,1)} async-done(((bf16[16,64,1024]{2,1,0:T(8,128)(2,1)}), bf16[16,64,1024]{2,1,0:T(8,128)(2,1)}, u32[]{:S(2)}, u32[]{:S(2)}) %all-to-all-start.1) | async-done | bytes 2097184 | tf_op jit(solution)/shard_map/all_to_all | solution.py:24
  182.3 2.7 %reduce_sum.22 = bf16[64,1024]{1,0:T(8,128)(2,1)} reduce(bf16[16,64,1024]{2,1,0:T(8,128)(2,1)} %all-to-all-done.1, bf16[]{:T(256)} %constant.3.clone.1), dimensions={0}, to_apply=%region_1.0 | reduce | flops 983040 | bytes 2228226 | tf_op jit(solution)/shard_map/reduce_sum | solution.py:25
  (11 shorter events, 0.0 us)
Async XLA Ops:
  7.2 127.8 %copy-start = (bf16[1024,896]{1,0:T(8,128)(2,1)S(1)}, bf16[1024,896]{1,0:T(8,128)(2,1)}, u32[]{:S(2)}) copy-start(bf16[1024,896]{1,0:T(8,128)(2,1)} %param.11) | copy-start | bytes 5505028
  7.2 57.3 %all-gather.3.cloned.1.call-start = ((), (), s32[]{:S(2)}) async-start(), calls=%async_computation.2 | async-start | bytes 4456448 | tf_op jit(solution)/shard_map/all_gather | solution.py:13
  9.1 125.9 %all-gather.5.cloned.1.call-start = ((), (), s32[]{:S(2)}) async-start(), calls=%async_computation.3 | async-start | bytes 6193152 | tf_op jit(solution)/shard_map/all_gather | solution.py:13
  69.0 29.0 %copy-start.1 = (bf16[128,896]{1,0:T(8,128)(2,1)S(1)}, bf16[128,896]{1,0:T(8,128)(2,1)}, u32[]{:S(2)}) copy-start(bf16[128,896]{1,0:T(8,128)(2,1)} %param.10) | copy-start | bytes 688132
  69.0 29.0 %copy-start.2 = (bf16[128,896]{1,0:T(8,128)(2,1)S(1)}, bf16[128,896]{1,0:T(8,128)(2,1)}, u32[]{:S(2)}) copy-start(bf16[128,896]{1,0:T(8,128)(2,1)} %param.9) | copy-start | bytes 688132
  134.9 4.0 %copy-start.4 = (bf16[1024,896]{1,0:T(8,128)(2,1)S(1)}, bf16[1024,896]{1,0:T(8,128)(2,1)}, u32[]{:S(2)}) copy-start(bf16[1024,896]{1,0:T(8,128)(2,1)} %param.12) | copy-start | bytes 5505028
  144.3 13.3 %slice-start = ((s8[5505024]{0:T(1024)(128)(4,1)}), s8[1310720]{0:T(1024)(128)(4,1)S(1)}, s32[]{:S(2)}) async-start(s8[5505024]{0:T(1024)(128)(4,1)} %bitcast.7), calls=%async_computation.4 | async-start | bytes 2621440
  144.3 38.0 %all-to-all-start.1 = ((bf16[16,64,1024]{2,1,0:T(8,128)(2,1)}), bf16[16,64,1024]{2,1,0:T(8,128)(2,1)}, u32[]{:S(2)}, u32[]{:S(2)}) async-start(bf16[16,64,1024]{2,1,0:T(8,128)(2,1)} %bitcast.5), calls=%async_computation.1 | async-start | bytes 4194304 | tf_op jit(solution)/shard_map/all_to_all | solution.py:24
  151.3 6.3 %slice-start.1 = ((s8[5505024]{0:T(1024)(128)(4,1)}), s8[4194304]{0:T(1024)(128)(4,1)S(1)}, s32[]{:S(2)}) async-start(s8[5505024]{0:T(1024)(128)(4,1)} %bitcast.7), calls=%async_computation.5 | async-start | bytes 8388608
  151.3 6.3 %copy-start.3 = (bf16[1024,2048]{1,0:T(8,128)(2,1)S(1)}, bf16[1024,2048]{1,0:T(8,128)(2,1)}, u32[]{:S(2)}) copy-start(bf16[1024,2048]{1,0:T(8,128)(2,1)} %all-gather.3.cloned.1.call-done) | copy-start | bytes 12582916
Sparse Core Ops, SparseCore 0:
  10.7 53.7 all-gather.2
  99.4 35.4 all-gather.4
where the time goes:
time: 192 us
  waiting for transfers between devices  107 us (56%)
  blocking collectives  28.8 us (15%)
  matrix products  28.6 us (15%)
  between operations  14.1 us (7%)
  starting transfers between devices  7.08 us (4%)
  other arithmetic  5.94 us (3%)
    all_gather x2, waiting for transfers between devices, in_one_piece(): lax.all_gather(both, axis, axis=dim, tiled=True)  91 us
    all_to_all x1, blocking collectives, sent_and_summed(): tiles = lax.all_to_all(cut_along(array, dim, peers), axis, 0, 0, tiled=True)  28.8 us
    all_to_all x1, waiting for transfers between devices, sent_and_summed(): tiles = lax.all_to_all(cut_along(array, dim, peers), axis, 0, 0, tiled=True)  16.2 us
    dot_general x3, matrix products, contract_first(): lax.dot_general(left, right, (((0,), (0,)), ((), ())), preferred_element_...  14.8 us
    dot_general x3, matrix products, contract_last(): lax.dot_general(left, right, (((1,), (1,)), ((), ())), preferred_element_...  13.8 us
    all_to_all x1, starting transfers between devices, sent_and_summed(): tiles = lax.all_to_all(cut_along(array, dim, peers), axis, 0, 0, tiled=True)  7 us
  transfers between devices with their start and end apart: 3, of which 3 were waited for; matrix products, arithmetic and copies ran while one was open for 8% of the time, Pallas kernels for 0%

commit v1 on v0

v1 whole, which is shorter than its diff:
```python
import jax
import jax.numpy as jnp
from jax import lax
from jax.experimental import pallas as pl
from jax.experimental.pallas import tpu as pltpu
from jax.sharding import PartitionSpec as P

BF = jnp.bfloat16
F32 = jnp.float32
MESH = pl.DeviceIdType.MESH
N_COPIES = 160
SIDES = (1, -1)


def kernel(
    x_hbm, dy_hbm, g_hbm, u_hbm, wg_hbm, wu_hbm, wd_hbm,
    ig_out, gw_out, uw_out, dw_out,
    x_all, dy_all, g_all, u_all, wg, wu, wd,
    slope, silu, hidden,
    part, part_in, chip_sum, half_in, full_in,
    hg_all, gg, ug,
    q, r2, rf, s1, t1, t2, r2b, rfb,
    send_sem, recv_sem, load_sem,
):
    r = lax.axis_index("row")
    c = lax.axis_index("col")
    z, core = lax.div(r, 2), lax.rem(r, 2)
    x, y = lax.div(c, 4), lax.rem(c, 4)
    up4 = lambda a, d: lax.rem(a + (d + 4), 4)
    col = lambda dx, dy: up4(x, dx) * 4 + up4(y, dy)
    row = lambda dz: up4(z, dz) * 2 + core
    row_other = lambda dz: up4(z, dz) * 2 + (1 - core)
    partner = {"row": row_other(0), "col": c}
    z_dev = lambda s: {"row": row(s), "col": c}

    loads = {}
    for i, (name, src, dst) in enumerate((
        ("dy", dy_hbm, dy_all.at[c]), ("g", g_hbm, g_all.at[r]), ("u", u_hbm, u_all.at[r]),
        ("wd", wd_hbm, wd), ("x", x_hbm, x_all.at[c]), ("wg", wg_hbm, wg), ("wu", wu_hbm, wu),
    )):
        loads[name] = pltpu.make_async_copy(src, dst, load_sem.at[i])
        loads[name].start()

    barrier = pltpu.get_barrier_semaphore()
    peers = [partner, z_dev(1), z_dev(-1)]
    peers += [{"row": r, "col": col(s, 0)} for s in SIDES]
    peers += [{"row": r, "col": col(0, s)} for s in SIDES]
    for p in peers:
        pl.semaphore_signal(barrier, inc=1, device_id=p, device_id_type=MESH)
    pl.semaphore_wait(barrier, len(peers))

    sent = []

    def send(src, dst, dev):
        i = len(sent)
        copy = pltpu.make_async_remote_copy(
            src_ref=src, dst_ref=dst, send_sem=send_sem.at[i], recv_sem=recv_sem.at[i],
            device_id=dev, device_id_type=MESH,
        )
        copy.start()
        sent.append(copy)
        return copy

    rows = (pl.ds(0, 32), pl.ds(32, 32))
    side_cols = {1: pl.ds(0, 512), -1: pl.ds(512, 512)}

    def at(h, a, b):
        return col(a, b) if h == 0 else col(b, a)

    def nb(h, dim, s):
        return {"row": r, "col": at(h, s, 0) if dim == 0 else at(h, 0, s)}

    def gather_xy(src, buf):
        m1, m2, r1, r2_ = {}, {}, {}, {}
        for h in range(2):
            for s in SIDES:
                m1[h, s] = send(src.at[rows[h]], buf.at[c, rows[h]], nb(h, 0, s))
        for h in range(2):
            for s in SIDES:
                m2[h, 0, s] = send(src.at[rows[h]], buf.at[c, rows[h]], nb(h, 1, s))
        yield
        for s in SIDES:
            for h in range(2):
                m1[h, s].wait_recv()
                slot = buf.at[at(h, -s, 0), rows[h]]
                piece = buf.at[at(h, -s, 0), rows[h], side_cols[s]]
                r1[h, s] = send(piece, piece, nb(h, 0, s))
                for t in SIDES:
                    m2[h, -s, t] = send(slot, slot, nb(h, 1, t))
                yield
        def relay(h, j, s):
            m2[h, j, s].wait_recv()
            piece = buf.at[at(h, j, -s), rows[h], side_cols[s]]
            r2_[h, j, s] = send(piece, piece, nb(h, 1, s))
        for h in range(2):
            for s in SIDES:
                relay(h, 0, s)
            yield
        for h in range(2):
            r1[h, 1].wait_recv()
            r1[h, -1].wait_recv()
            slot = buf.at[at(h, 2, 0), rows[h]]
            for t in SIDES:
                m2[h, 2, t] = send(slot, slot, nb(h, 1, t))
            yield
        for j in (-1, 1, 2):
            for h in range(2):
                for s in SIDES:
                    relay(h, j, s)
                yield
        for h in range(2):
            for j in (0, -1, 1, 2):
                for s in SIDES:
                    r2_[h, j, s].wait_recv()

    z_half = {1: pl.ds(0, 64), -1: pl.ds(64, 64)}

    def gather_z(src, buf, done):
        mine = buf.at[r]
        p0 = send(src, mine, partner)
        m = {s: send(src, mine, z_dev(s)) for s in SIDES}
        yield
        p0.wait_recv()
        done(0)
        yield
        rl, fw = {}, {}
        for s in SIDES:
            m[s].wait_recv()
            piece = buf.at[row(-s), z_half[s]]
            rl[s] = send(piece, piece, z_dev(s))
            fw[s] = send(buf.at[row(-s)], buf.at[row(-s)], partner)
            yield
        for s in SIDES:
            fw[s].wait_recv()
            done(-s)
            yield
        rl[1].wait_recv()
        rl[-1].wait_recv()
        far = send(buf.at[row(2)], buf.at[row(2)], partner)
        yield
        far.wait_recv()
        done(2)

    def factors(dz):
        first = up4(z, dz) * 2

        @pl.loop(0, 8)
        def _(i):
            slot = first + lax.div(i, 4)
            at_rows = pl.ds(lax.rem(i, 4) * 32, 32)
            gate = g_all[slot, at_rows, :].astype(F32)
            upv = u_all[slot, at_rows, :].astype(F32)
            sigma = 1.0 / (1.0 + jnp.exp(-gate))
            si = gate * sigma
            hidden[slot, at_rows, :] = (si * upv).astype(BF)
            silu[slot, at_rows, :] = si
            slope[slot, at_rows, :] = upv * sigma * (1.0 + gate * (1.0 - sigma))

    nothing = lambda dz: None

    def drain(gen):
        for _ in gen:
            pass

    ag_dy = gather_xy(dy_hbm, dy_all)
    next(ag_dy)
    ag_g = gather_z(g_hbm, g_all, nothing)
    next(ag_g)
    ag_u = gather_z(u_hbm, u_all, nothing)
    next(ag_u)
    loads["g"].wait()
    loads["u"].wait()
    next(ag_g)
    next(ag_u)
    factors(0)
    for _ in range(4):
        next(ag_dy)
    live = [ag_g, ag_u]
    k = 0
    for _ in ag_dy:
        if k % 2 == 0:
            next(live[0], None)
            next(live[1], None)
        k += 1
    loads["dy"].wait()
    loads["wd"].wait()

    ag_x = gather_xy(x_hbm, x_all)
    next(ag_x)

    zs = (2, 1, -1, 0)
    ps = {}
    for i, dz in enumerate(zs):
        first = up4(z, dz) * 4
        left = dy_all[pl.ds(first, 4)].reshape(256, 1024)
        prod = lax.dot_general(left, wd[...], (((1,), (1,)), ((), ())), preferred_element_type=F32)
        part[i] = prod.astype(BF).reshape(2, 128, 896)
        ps[dz] = send(part.at[i, 1 - core], part_in.at[i], partner)
        if i:
            next(ag_x)

    def chip(i, at_rows):
        return part[i, core, at_rows, :].astype(F32) + part_in[i, at_rows, :].astype(F32)

    drain(ag_g)
    drain(ag_u)
    ps[2].wait_recv()

    @pl.loop(0, 4)
    def _(k):
        at_rows = pl.ds(k * 32, 32)
        chip_sum[0, at_rows, :] = chip(0, at_rows).astype(BF)

    hs = {s: send(chip_sum.at[0, z_half[s]], half_in.at[z_half[s]], z_dev(s)) for s in SIDES}
    factors(-1)
    next(ag_x)
    fs = {}
    for n, s in enumerate(SIDES):
        ps[s].wait_recv()
        hs[s].wait_recv()
        lo = z_half[s].start

        @pl.loop(0, 4)
        def _(k):
            at_rows = pl.ds(k * 32, 32)
            chip_sum[1 + n, at_rows, :] = chip(1 + n, at_rows).astype(BF)

        @pl.loop(0, 2)
        def _(k):
            at_rows = pl.ds(lo + k * 32, 32)
            both = chip(1 + n, at_rows) + half_in[at_rows, :].astype(F32)
            chip_sum[1 + n, at_rows, :] = both.astype(BF)

        fs[s] = send(chip_sum.at[1 + n], full_in.at[n], z_dev(s))
    next(ag_x, None)
    factors(1)
    next(ag_x, None)
    factors(2)
    next(ag_x, None)
    ps[0].wait_recv()
    fs[1].wait_recv()
    fs[-1].wait_recv()

    @pl.loop(0, 4)
    def _(k):
        at_rows = pl.ds(k * 32, 32)
        total = chip(3, at_rows) + full_in[0, at_rows, :].astype(F32) + full_in[1, at_rows, :].astype(F32)
        hg_all[r, at_rows, :] = total.astype(BF)

    a2, a1 = {}, {}

    def stage1_far(h, b, slot):
        for s in SIDES:
            a2[h, b, s] = send(
                q.at[slot, rows[h], side_cols[s]], r2.at[h, b, :, side_cols[s]], e_nb(h, 0, s)
            )

    def e_nb(h, dim, s):
        return nb(1 - h, dim, s)

    def e_at(h, a, b_abs):
        return b_abs * 4 + up4(y, a) if h == 0 else up4(x, a) * 4 + b_abs

    def input_grad_block(dz):
        tb = up4(z, dz)

        @pl.loop(0, 8)
        def _(i):
            slot = tb * 2 + lax.div(i, 4)
            at_rows = pl.ds(lax.rem(i, 4) * 32, 32)
            hg = hg_all[slot, at_rows, :].astype(F32)
            gg[slot, at_rows, :] = (hg * slope[slot, at_rows, :]).astype(BF)
            ug[slot, at_rows, :] = (hg * silu[slot, at_rows, :]).astype(BF)

        nt = (((1,), (1,)), ((), ()))
        left_g = gg[pl.ds(tb * 2, 2)].reshape(256, 896)
        left_u = ug[pl.ds(tb * 2, 2)].reshape(256, 896)
        prod = lax.dot_general(left_g, wg[...], nt, preferred_element_type=F32)
        prod = prod + lax.dot_general(left_u, wu[...], nt, preferred_element_type=F32)
        q[pl.ds(tb * 4, 4)] = prod.astype(BF).reshape(4, 64, 1024)
        i = (0, -1, 1, 2).index(dz)
        for s in SIDES:
            a2[0, i, s] = send(
                q.at[e_at(0, 2, tb), rows[0], side_cols[s]],
                r2.at[0, i, :, side_cols[s]],
                e_nb(0, 0, s),
            )

    scale = float(x_all.shape[0] * x_all.shape[1]) ** -0.5
    tn = (((0,), (0,)), ((), ()))

    def down_grad(lo, n):
        left = hidden[:, :, lo : lo + n].reshape(1024, n)
        dw_out[lo : lo + n, :] = scale * lax.dot_general(
            left, dy_all[...].reshape(1024, 1024), tn, preferred_element_type=F32
        )

    def weight_grad(which, k):
        left = x_all[:, :, k * 256 : (k + 1) * 256].reshape(1024, 256)
        src, dst = (gg, gw_out) if which == 0 else (ug, uw_out)
        dst[k * 256 : (k + 1) * 256, :] = scale * lax.dot_general(
            left, src[...].reshape(1024, 896), tn, preferred_element_type=F32
        )

    loads["wg"].wait()
    loads["wu"].wait()
    ag_h = gather_z(hg_all.at[r], hg_all, input_grad_block)
    next(ag_h)
    down_grad(0, 384)
    next(ag_x, None)
    next(ag_h)
    next(ag_h)
    next(ag_h)
    next(ag_x, None)
    next(ag_x, None)
    down_grad(384, 512)
    next(ag_x, None)
    next(ag_x, None)
    next(ag_h)
    next(ag_h)
    next(ag_h)
    next(ag_x, None)
    next(ag_x, None)
    drain(ag_h)

    def q_rows(h, a, b_abs, cols=slice(None)):
        return q[e_at(h, a, b_abs), rows[h], cols].astype(F32)

    for j in range(4):
        for s in SIDES:
            a2[1, j, s] = send(
                q.at[e_at(1, 2, j), rows[1], side_cols[s]], r2.at[1, j, :, side_cols[s]], e_nb(1, 0, s)
            )
    drain(ag_x)
    loads["x"].wait()
    order_a = (0, -1, 1, 2)

    def b_abs(h, i):
        return up4(z, order_a[i]) if h == 0 else i

    a_sum = {}

    def near(h, i):
        for n, s in enumerate(SIDES):
            a2[h, i, s].wait_recv()
            sc, oc = side_cols[s], side_cols[-s]
            s1[h, i, n, :, sc] = (q_rows(h, s, b_abs(h, i), sc) + r2[h, i, :, sc].astype(F32)).astype(BF)
            s1[h, i, n, :, oc] = q[e_at(h, s, b_abs(h, i)), rows[h], oc]
            a1[h, i, s] = send(s1.at[h, i, n], rf.at[h, i, n], e_nb(h, 0, s))

    def mine(h, i):
        for s in SIDES:
            a1[h, i, s].wait_recv()
        b = b_abs(h, i)
        t1[h, b] = (
            q_rows(h, 0, b) + rf[h, i, 0].astype(F32) + rf[h, i, 1].astype(F32)
        ).astype(BF)

    for i in range(4):
        near(0, i)
    weight_grad(0, 0)
    for i in range(4):
        near(1, i)
    weight_grad(0, 1)
    weight_grad(0, 2)
    weight_grad(0, 3)
    c2, c1 = {}, {}
    own2 = (x, y)
    for h in range(2):
        for i in range(4):
            mine(h, i)
        for s in SIDES:
            far = up4(own2[h], 2)
            c2[h, s] = send(t1.at[h, far, :, side_cols[s]], r2b.at[h, :, side_cols[s]], e_nb(h, 1, s))
    weight_grad(1, 0)
    weight_grad(1, 1)
    for h in range(2):
        for n, s in enumerate(SIDES):
            c2[h, s].wait_recv()
            b = up4(own2[h], s)
            sc, oc = side_cols[s], side_cols[-s]
            t2[h, n, :, sc] = (t1[h, b, :, sc].astype(F32) + r2b[h, :, sc].astype(F32)).astype(BF)
            t2[h, n, :, oc] = t1[h, b, :, oc]
            c1[h, s] = send(t2.at[h, n], rfb.at[h, n], e_nb(h, 1, s))
    weight_grad(1, 2)
    weight_grad(1, 3)
    for h in range(2):
        for s in SIDES:
            c1[h, s].wait_recv()
        ig_out[rows[h], :] = (
            t1[h, own2[h]].astype(F32) + rfb[h, 0].astype(F32) + rfb[h, 1].astype(F32)
        ).astype(BF)
    for copy in sent:
        copy.wait_send()


def shards(layer_input, out_grad, gate_saved, up_saved, gate_weight, up_weight, down_weight):
    any_ = pl.BlockSpec(memory_space=pl.ANY)
    vm = pl.BlockSpec(memory_space=pltpu.VMEM)
    V = pltpu.VMEM
    return pl.pallas_call(
        kernel,
        out_shape=OUT_SHAPES,
        in_specs=[any_] * 7,
        out_specs=(vm,) * 4,
        scratch_shapes=[
            V((16, 64, 1024), BF), V((16, 64, 1024), BF),
            V((8, 128, 896), BF), V((8, 128, 896), BF),
            V((1024, 896), BF), V((1024, 896), BF), V((896, 1024), BF),
            V((8, 128, 896), F32), V((8, 128, 896), F32), V((8, 128, 896), BF),
            V((4, 2, 128, 896), BF), V((4, 128, 896), BF), V((3, 128, 896), BF),
            V((128, 896), BF), V((2, 128, 896), BF),
            V((8, 128, 896), BF), V((8, 128, 896), BF), V((8, 128, 896), BF),
            V((16, 64, 1024), BF),
            V((2, 4, 32, 1024), BF), V((2, 4, 2, 32, 1024), BF), V((2, 4, 2, 32, 1024), BF),
            V((2, 4, 32, 1024), BF), V((2, 2, 32, 1024), BF),
            V((2, 32, 1024), BF), V((2, 2, 32, 1024), BF),
            pltpu.SemaphoreType.DMA((N_COPIES,)),
            pltpu.SemaphoreType.DMA((N_COPIES,)),
            pltpu.SemaphoreType.DMA((7,)),
        ],
        compiler_params=pltpu.CompilerParams(
            collective_id=0, has_side_effects=True, vmem_limit_bytes=VLIM
        ),
        name="swiglu_backward",
    )(layer_input, out_grad, gate_saved, up_saved, gate_weight, up_weight, down_weight)


VLIM = 66_000_000
OUT_SHAPES = (
    jax.ShapeDtypeStruct((64, 1024), BF),
    jax.ShapeDtypeStruct((1024, 896), F32),
    jax.ShapeDtypeStruct((1024, 896), F32),
    jax.ShapeDtypeStruct((896, 1024), F32),
)


def solution(mesh):
    placed = (
        P("col", "row"), P("col", "row"), P("row", "col"), P("row", "col"),
        P("row", "col"), P("row", "col"), P("col", "row"),
    )
    return jax.shard_map(
        shards,
        mesh=mesh,
        in_specs=placed,
        out_specs=(P("col", "row"), P("row", "col"), P("row", "col"), P("col", "row")),
        check_vma=False,
    )
```

time: 192 us -> 98.5 us (0.51)
  waiting for transfers between devices: 107 us -> 0 us
  Pallas kernels: 0 us -> 86.6 us
  blocking collectives: 28.8 us -> 0 us
  matrix products: 28.6 us -> 0 us
  between operations: 14.1 us -> 0.65 us
  local copies, waits for them, and re-layouts: 0.04 us -> 11 us
  starting transfers between devices: 7.08 us -> 0 us
  other arithmetic: 5.94 us -> 0 us
    all_gather x2 -> x0, waiting for transfers between devices: 91 us -> none  [in_one_piece(): lax.all_gather(both, axis, axis=dim, tiled=True)]
    pallas_call x0 -> x1, Pallas kernels: none -> 86.6 us  [shards(): pl.pallas_call(kernel, out_shape=OUT_SHAPES, in_specs=[any_] * 7, out_spe...]
    all_to_all x1 -> x0, blocking collectives: 28.8 us -> none  [sent_and_summed(): tiles = lax.all_to_all(cut_along(array, dim, peers), axis, 0, 0, tiled=True)]
    dot_general x6 -> x0, matrix products: 28.6 us -> none  [the longest x3 14.8 us: contract_first(): lax.dot_general(left, right, (((0,), (0,)), ((), ())), preferred_element_...]
    all_to_all x1 -> x0, waiting for transfers between devices: 16.2 us -> none  [sent_and_summed(): tiles = lax.all_to_all(cut_along(array, dim, peers), axis, 0, 0, tiled=True)]
    unnamed x14 -> x8, local copies, waits for them, and re-layouts: 0.04 us -> 11 us
    all_to_all x1 -> x0, starting transfers between devices: 7 us -> none  [sent_and_summed(): tiles = lax.all_to_all(cut_along(array, dim, peers), axis, 0, 0, tiled=True)]
    reduce_sum x2 -> x0, other arithmetic: 2.92 us -> none  [sent_and_summed(): return jnp.sum(tiles.astype(jnp.float32), axis=0)]
  transfers between devices with their start and end apart: 3 -> 0, of which waited for: 3 -> 0; matrix products, arithmetic and copies ran while one was open for 8% -> 0% of each run, Pallas kernels for 0% -> 0%
where the time goes in v1:
time: 98.5 us; the launch traced here: 98.3 us
  Pallas kernels  86.6 us (88%)
  local copies, waits for them, and re-layouts  11 us (11%)
    pallas_call x1, Pallas kernels, shards(): pl.pallas_call(kernel, out_shape=OUT_SHAPES, in_specs=[any_] * 7, out_spe...  86.6 us
    unnamed x8, local copies, waits for them, and re-layouts  11 us

profile of v1, /device:TPU:0, one launch (start us, length us, event | category | flops | bytes accessed | tf_op | source)
XLA Modules:
  0.0 98.3 jit_solution(5130365833192414535)
XLA Ops:
  0.6 86.6 %swiglu_backward.1 = (bf16[64,1024]{1,0:T(8,128)(2,1)}, f32[1024,896]{1,0:T(8,128)}, f32[1024,896]{1,0:T(8,128)}, f32[896,1024]{1,0:T(8,128)}) custom-call(bf16[64,1024]{1,0:T(8,128)(2,1)} %x_hbm.1, bf16[64,1024]{1,0:T(8,128)(2,1)} %dy_hbm.1, bf16[128,896]{1,0:T(8,128)(2,1)} %g_hbm.1, bf16[128,896]{1,0:T(8,128)(2,1)} %u_hbm.1, bf16[1024,896]{1,0:T(8,128)(2,1)} %wg_hbm.1, ...), custom_call_target="tpu_custom_call" | custom-call | tf_op jit(solution)/shard_map/swiglu_backward/pallas_call | solution.py:401
  87.3 1.6 %copy.15 = bf16[64,1024]{1,0:T(8,128)(2,1)} copy(bf16[64,1024]{1,0:T(8,128)(2,1)} %get-tuple-element.8) | data formatting | bytes 262144
  88.8 0.0 copy-start.1
  88.8 4.3 %copy.16 = f32[1024,896]{1,0:T(8,128)} copy(f32[1024,896]{1,0:T(8,128)} %get-tuple-element.9) | data formatting | bytes 7340032
  93.1 0.0 copy-done.1
  93.1 0.0 copy-start
  93.1 1.9 %copy.17 = f32[1024,896]{1,0:T(8,128)} copy(f32[1024,896]{1,0:T(8,128)S(1)} %copy-done.1) | data formatting | bytes 7340032
  95.0 1.5 %copy-done = f32[896,1024]{1,0:T(8,128)S(1)} copy-done((f32[896,1024]{1,0:T(8,128)S(1)}, f32[896,1024]{1,0:T(8,128)}, u32[]{:S(2)}) %copy-start) | copy-done | bytes 3670040
  96.5 1.8 %copy.18 = f32[896,1024]{1,0:T(8,128)} copy(f32[896,1024]{1,0:T(8,128)S(1)} %copy-done) | data formatting | bytes 7340032
Async XLA Ops:
  88.8 4.3 %copy-start.1 = (f32[1024,896]{1,0:T(8,128)S(1)}, f32[1024,896]{1,0:T(8,128)}, u32[]{:S(2)}) copy-start(f32[1024,896]{1,0:T(8,128)} %get-tuple-element.10) | copy-start | bytes 11010052
  93.1 3.4 %copy-start = (f32[896,1024]{1,0:T(8,128)S(1)}, f32[896,1024]{1,0:T(8,128)}, u32[]{:S(2)}) copy-start(f32[896,1024]{1,0:T(8,128)} %get-tuple-element.11) | copy-start | bytes 11010052
